TPU v7x, 32 devices: a whole 2x2x4 slice. The times are simulated.
32 devices in a mesh: section: 4 (over z), tensor: 8 (over y, x, core).
Axes of the slice: x: 2, y: 2, z: 4, core: 2. Of those that a mesh axis runs over, the one named last changes fastest.
Arguments:
- resid: bfloat16 [32, 3584], P('tensor'), may hold values from -6 to 6
- w_enc: bfloat16 [7168, 3584], P(('section', 'tensor')), may hold values from -0.09375 to 0.09375
- b_enc: float32 [7168], P(('section', 'tensor')), may hold values from -1 to 0.5
- w_dec: bfloat16 [7168, 3584], P(('section', 'tensor')), may hold values from -0.0625 to 0.0625
- b_dec: float32 [3584], replicated, may hold values from -3 to 3
Outputs:
- recon: float32 [32, 3584], P('tensor')
- grad_w_dec: bfloat16 [7168, 3584], P(('section', 'tensor'))
- code_grad: float32 [32, 7168], P(None, ('section', 'tensor'))
- grad_b_dec: float32 [3584], replicated
- loss_value: float32 [], replicated
All inputs are finite; a program needn't handle non-finite values.
Results may differ from a plain program's by a relative error of at most 0.0032.
The roundings to bfloat16 on the way count: a program that leaves them out, or rounds other values in their place, can miss the bound.
Values may be sent and summed in bfloat16 or wider, within the bound.
No kernel may reach another device: no remote copies, remote signals or barrier semaphores. Data moves between devices by JAX's collectives and lax.ppermute only.
A program may use at most 64 MiB of HBM per device.

v0:
```python
import jax
import jax.numpy as jnp
from jax import lax
from jax.sharding import PartitionSpec as P

epsilon = 1e-06


def per_device(resid, w_enc, b_enc, w_dec, b_dec):
    stream = lax.all_gather(resid, "tensor", axis=0, tiled=True)
    preact = (
        lax.dot_general(stream, w_enc, (((1,), (1,)), ((), ())), preferred_element_type=jnp.float32)
        + b_enc
    )
    codes = jnp.maximum(preact, 0.0).astype(jnp.bfloat16)
    codes_f32 = codes.astype(jnp.float32)
    dec_f32 = w_dec.astype(jnp.float32)
    dec_norm = jnp.sqrt(jnp.sum(dec_f32 * dec_f32, axis=1) + epsilon)
    penalty = lax.psum(jnp.sum(codes_f32 * dec_norm), ("section", "tensor"))
    total_rows = stream.shape[0]
    model_width = stream.shape[1]
    shares = lax.psum_scatter(
        jnp.dot(codes, w_dec, preferred_element_type=jnp.float32),
        "tensor",
        scatter_dimension=0,
        tiled=True,
    )
    shares = lax.psum(shares, "section")
    recon = shares + b_dec
    errors = recon - resid.astype(jnp.float32)
    squares, grad_b_dec = lax.psum((jnp.sum(errors * errors), jnp.sum(errors, axis=0)), "tensor")
    err_half = lax.all_gather(errors.astype(jnp.bfloat16), "tensor", axis=0, tiled=True)
    loss_value = (0.5 * squares + penalty) / (total_rows * model_width)
    code_sums = jnp.sum(codes_f32, axis=0)
    grad_w_dec = lax.dot_general(
        codes, err_half, (((0,), (0,)), ((), ())), preferred_element_type=jnp.float32
    )
    grad_w_dec = grad_w_dec + code_sums[:, None] * dec_f32 / dec_norm[:, None]
    code_grad = (
        lax.dot_general(
            err_half, w_dec, (((1,), (1,)), ((), ())), preferred_element_type=jnp.float32
        )
        + dec_norm
    )
    return (recon, grad_w_dec.astype(jnp.bfloat16), code_grad, grad_b_dec, loss_value)


def solution(mesh):
    in_specs = (
        P("tensor", None),
        P(("section", "tensor"), None),
        P(("section", "tensor")),
        P(("section", "tensor"), None),
        P(),
    )
    out_specs = (
        P("tensor", None),
        P(("section", "tensor"), None),
        P(None, ("section", "tensor")),
        P(),
        P(),
    )
    return jax.shard_map(
        per_device, mesh=mesh, in_specs=in_specs, out_specs=out_specs, check_vma=False
    )
```

profile of v0, /device:TPU:0, one launch (start us, length us, event | category | flops | bytes accessed | tf_op | source)
XLA Modules:
  0.0 148.7 jit_solution(17115211651597049739)
XLA Ops:
  7.2 0.0 copy-start
  7.2 0.0 copy-start.2
  7.2 0.0 copy-start.6
  7.2 0.0 all-reduce.4.cloned.1.call-start
  7.2 1.9 %fusion.2 = f32[224]{0:T(256)S(1)} fusion(bf16[224,3584]{1,0:T(8,128)(2,1)} %param.8), kind=kLoop, calls=%fused_computation.5 | loop fusion | flops 2408224 | bytes 1606528 | tf_op jit(solution)/shard_map/reduce_sum | solution.py:18
  9.2 0.0 copy-start.1
  9.2 0.0 copy-done.2
  9.2 12.0 %all-gather = bf16[8,4,3584]{2,1,0:T(4,128)(2,1)} all-gather(bf16[1,4,3584]{2,1,0:T(4,128)(2,1)S(1)} %bitcast.12), channel_id=1, replica_groups=mesh['section'=4,'tensor'=8] {'tensor'}, dimensions={0}, use_global_device_ids=true | all-gather | bytes 258048 | tf_op jit(solution)/shard_map/all_gather | solution.py:10
  21.2 1.0 reshape.22
  22.2 0.0 copy-done
  22.2 0.0 copy-done.6
  22.2 1.2 fusion.5
  23.4 0.0 copy-start.7
  23.4 0.0 copy-start.5
  23.4 0.0 copy-done.1
  23.4 1.2 fusion.7
  24.5 0.0 all-reduce.4.cloned.1.call-update
  24.5 39.9 %psum.31 = f32[]{:T(128)} all-reduce(f32[]{:T(128)} %get-tuple-element.7), channel_id=1, replica_groups=mesh['section'=4,'tensor'=8] {'section','tensor'}, use_global_device_ids=true, to_apply=%region_9.0 | all-reduce | flops 1 | bytes 8 | tf_op jit(solution)/shard_map/psum | solution.py:19
  64.4 0.0 copy-done.7
  64.4 0.6 dynamic-slice
  65.7 14.0 %all-reduce.4.cloned.1.call-done = f32[32,3584]{1,0:T(8,128)} async-done(((f32[32,3584]{1,0:T(8,128)}), f32[32,3584]{1,0:T(8,128)}) %all-reduce.4.cloned.1.call-update) | async-done | bytes 458768
  79.7 0.9 constant_dynamic-slice_fusion
  80.6 19.6 %psum.28 = f32[4,3584]{1,0:T(4,128)S(1)} all-reduce(f32[4,3584]{1,0:T(4,128)S(1)} %constant_dynamic-slice_fusion), channel_id=1, replica_groups=mesh['section'=4,'tensor'=8] {'section'}, use_global_device_ids=true, to_apply=%region_1.0 | all-reduce | flops 14336 | bytes 114688 | tf_op jit(solution)/shard_map/psum | solution.py:28
  100.2 0.0 copy-done.5
  100.2 0.7 multiply_reduce_fusion
  101.0 9.6 %all-gather.1 = bf16[8,4,3584]{2,1,0:T(4,128)(2,1)} all-gather(bf16[1,4,3584]{2,1,0:T(4,128)(2,1)S(1)} %convert_bitcast_fusion), channel_id=1, replica_groups=mesh['section'=4,'tensor'=8] {'tensor'}, dimensions={0}, use_global_device_ids=true | all-gather | bytes 258048 | tf_op jit(solution)/shard_map/all_gather | solution.py:32
  110.6 1.0 reshape.24
  111.6 1.2 convolution_add_fusion.1
  112.8 1.8 %fusion = bf16[224,3584]{1,0:T(8,128)(2,1)} fusion(bf16[32,224]{1,0:T(8,128)(2,1)S(1)} %get-tuple-element.12, bf16[32,3584]{1,0:T(8,128)(2,1)S(1)} %reshape.24, bf16[224,3584]{1,0:T(8,128)(2,1)S(1)} %copy-done.1, f32[224]{0:T(256)S(1)} %add_sqrt_fusion, f32[224]{0:T(256)S(1)} %get-tuple-element.8), kind=kOutput, calls=%fused_computation.1 | convolution fusion | flops 55394304 | bytes 3456768 | tf_op jit(solution)/shard_map/dot_general | solution.py:35
  114.6 0.0 copy-done.3
  114.6 0.0 copy-done.4
  114.6 24.8 %all-reduce.1 = (f32[3584]{0:T(1024)}, f32[]{:T(128)}) all-reduce(f32[3584]{0:T(1024)S(1)} %copy-done.4, f32[]{:T(128)} %get-tuple-element.5), channel_id=1, replica_groups=mesh['section'=4,'tensor'=8] {'tensor'}, use_global_device_ids=true, to_apply=%region_5.0 | all-reduce | flops 3585 | bytes 28680 | tf_op jit(solution)/shard_map/psum | solution.py:31
  (4 shorter events, 0.0 us)
Async XLA Ops:
  7.2 15.0 %copy-start = (bf16[224,3584]{1,0:T(8,128)(2,1)S(1)}, bf16[224,3584]{1,0:T(8,128)(2,1)}, u32[]{:S(2)}) copy-start(bf16[224,3584]{1,0:T(8,128)(2,1)} %param.6) | copy-start | bytes 4816900
  7.2 2.0 %copy-start.2 = (bf16[4,3584]{1,0:T(4,128)(2,1)S(1)}, bf16[4,3584]{1,0:T(4,128)(2,1)}, u32[]{:S(2)}) copy-start(bf16[4,3584]{1,0:T(4,128)(2,1)} %param.5) | copy-start | bytes 86020
  7.2 15.0 %copy-start.6 = (f32[224]{0:T(256)S(1)}, f32[224]{0:T(256)}, u32[]{:S(2)}) copy-start(f32[224]{0:T(256)} %param.7) | copy-start | bytes 2692
  7.2 72.5 %all-reduce.4.cloned.1.call-start = ((), (), s32[]{:S(2)}) async-start(), calls=%async_computation | async-start | bytes 917504
  9.2 14.2 %copy-start.1 = (bf16[224,3584]{1,0:T(8,128)(2,1)S(1)}, bf16[224,3584]{1,0:T(8,128)(2,1)}, u32[]{:S(2)}) copy-start(bf16[224,3584]{1,0:T(8,128)(2,1)} %param.8) | copy-start | bytes 4816900
  23.4 41.1 %copy-start.7 = (u32[32]{0:T(128)S(1)}, u32[32]{0:T(128)}, u32[]{:S(2)}) copy-start(u32[32]{0:T(128)} %constant.13) | copy-start | bytes 388
  23.4 76.8 %copy-start.5 = (f32[3584]{0:T(1024)S(1)}, f32[3584]{0:T(1024)}, u32[]{:S(2)}) copy-start(f32[3584]{0:T(1024)} %param.9) | copy-start | bytes 43012
  100.9 13.6 %copy-start.3 = (f32[4,3584]{1,0:T(4,128)}, f32[4,3584]{1,0:T(4,128)S(1)}, u32[]{:S(2)}) copy-start(f32[4,3584]{1,0:T(4,128)S(1)} %get-tuple-element.11) | copy-start | bytes 172036
  112.8 1.8 %copy-start.4 = (f32[3584]{0:T(1024)S(1)}, f32[3584]{0:T(1024)}, u32[]{:S(2)}) copy-start(f32[3584]{0:T(1024)} %get-tuple-element.6) | copy-start | bytes 43012
Sparse Core Ops, SparseCore 0:
  24.7 54.9 all-reduce.3
where the time goes:
time: 149 us
  blocking collectives  106 us (71%)
  between operations  17.2 us (12%)
  waiting for transfers between devices  14 us (9%)
  matrix products  5.33 us (4%)
  local copies, waits for them, and re-layouts  3.52 us (2%)
  other arithmetic  2.7 us (2%)
    psum x1, blocking collectives, per_device(): penalty = lax.psum(jnp.sum(codes_f32 * dec_norm), ('section', 'tensor'))  39.9 us
    psum x1, blocking collectives, per_device(): lax.psum((jnp.sum(errors * errors), jnp.sum(errors, axis=0)), 'tensor')  24.8 us
    psum x1, blocking collectives, per_device(): shares = lax.psum(shares, 'section')  19.6 us
    unnamed x2, waiting for transfers between devices  14 us
    all_gather x1, blocking collectives, per_device(): stream = lax.all_gather(resid, 'tensor', axis=0, tiled=True)  12 us
    all_gather x1, blocking collectives, per_device(): lax.all_gather(errors.astype(jnp.bfloat16), 'tensor', axis=0, tiled=True)  9.61 us
    unnamed x20, local copies, waits for them, and re-layouts  3.52 us
  transfers between devices with their start and end apart: 1, of which 1 were waited for; matrix products, arithmetic and copies ran while one was open for 0% of the time, Pallas kernels for 0%

commit v1 on v0

--- a/solution.py
+++ b/solution.py
@@ -25,7 +25,7 @@
         scatter_dimension=0,
         tiled=True,
     )
-    shares = lax.psum(shares, "section")
+    shares = jnp.sum(lax.all_gather(shares, "section"), axis=0)
     recon = shares + b_dec
     errors = recon - resid.astype(jnp.float32)
     squares, grad_b_dec = lax.psum((jnp.sum(errors * errors), jnp.sum(errors, axis=0)), "tensor")

time: 149 us -> 144 us (0.966)
  blocking collectives: 106 us -> 100 us
    psum x1 -> x0, blocking collectives: 19.6 us -> none  [per_device(): shares = lax.psum(shares, 'section')]
    all_gather x0 -> x1, blocking collectives: none -> 13.8 us  [per_device(): shares = jnp.sum(lax.all_gather(shares, 'section'), axis=0)]
    unnamed x20 -> x18, local copies, waits for them, and re-layouts: 3.52 us -> 3.52 us
where the time goes in v1:
time: 144 us
  blocking collectives  100 us (69%)
  between operations  17.2 us (12%)
  waiting for transfers between devices  14 us (10%)
  matrix products  5.33 us (4%)
  local copies, waits for them, and re-layouts  3.52 us (2%)
  other arithmetic  3.47 us (2%)
    psum x1, blocking collectives, per_device(): penalty = lax.psum(jnp.sum(codes_f32 * dec_norm), ('section', 'tensor'))  39.9 us
    psum x1, blocking collectives, per_device(): lax.psum((jnp.sum(errors * errors), jnp.sum(errors, axis=0)), 'tensor')  24.8 us
    unnamed x2, waiting for transfers between devices  14 us
    all_gather x1, blocking collectives, per_device(): shares = jnp.sum(lax.all_gather(shares, 'section'), axis=0)  13.8 us
    all_gather x1, blocking collectives, per_device(): stream = lax.all_gather(resid, 'tensor', axis=0, tiled=True)  12 us
    all_gather x1, blocking collectives, per_device(): lax.all_gather(errors.astype(jnp.bfloat16), 'tensor', axis=0, tiled=True)  9.52 us
    unnamed x18, local copies, waits for them, and re-layouts  3.52 us
  transfers between devices with their start and end apart: 1, of which 1 were waited for; matrix products, arithmetic and copies ran while one was open for 0% of the time, Pallas kernels for 0%

profile of v1, /device:TPU:0, one launch (start us, length us, event | category | flops | bytes accessed | tf_op | source)
XLA Modules:
  0.0 143.6 jit_solution(724535026031730684)
XLA Ops:
  7.2 0.0 copy-start
  7.2 0.0 copy-start.2
  7.2 0.0 copy-start.5
  7.2 0.0 all-reduce.4.cloned.1.call-start
  7.2 1.9 %fusion.2 = f32[224]{0:T(256)S(1)} fusion(bf16[224,3584]{1,0:T(8,128)(2,1)} %param.8), kind=kLoop, calls=%fused_computation.5 | loop fusion | flops 2408224 | bytes 1606528 | tf_op jit(solution)/shard_map/reduce_sum | solution.py:18
  9.2 0.0 copy-start.1
  9.2 0.0 copy-done.2
  9.2 12.0 %all-gather.1 = bf16[8,4,3584]{2,1,0:T(4,128)(2,1)} all-gather(bf16[1,4,3584]{2,1,0:T(4,128)(2,1)S(1)} %bitcast.14), channel_id=1, replica_groups=mesh['section'=4,'tensor'=8] {'tensor'}, dimensions={0}, use_global_device_ids=true | all-gather | bytes 258048 | tf_op jit(solution)/shard_map/all_gather | solution.py:10
  21.2 1.0 reshape.23
  22.2 0.0 copy-done
  22.2 0.0 copy-done.5
  22.2 1.2 fusion.5
  23.4 0.0 copy-start.6
  23.4 0.0 copy-done.1
  23.4 1.2 fusion.7
  24.5 0.0 all-reduce.4.cloned.1.call-update
  24.5 39.9 %psum.23 = f32[]{:T(128)} all-reduce(f32[]{:T(128)} %get-tuple-element.7), channel_id=1, replica_groups=mesh['section'=4,'tensor'=8] {'section','tensor'}, use_global_device_ids=true, to_apply=%region_9.0 | all-reduce | flops 1 | bytes 8 | tf_op jit(solution)/shard_map/psum | solution.py:19
  64.4 0.0 copy-done.6
  64.4 0.6 dynamic-slice
  65.7 14.0 %all-reduce.4.cloned.1.call-done = f32[32,3584]{1,0:T(8,128)} async-done(((f32[32,3584]{1,0:T(8,128)}), f32[32,3584]{1,0:T(8,128)}) %all-reduce.4.cloned.1.call-update) | async-done | bytes 458768
  79.7 0.9 dynamic-slice_bitcast_fusion
  80.6 13.8 %all-gather.2 = f32[4,4,3584]{2,1,0:T(4,128)S(1)} all-gather(f32[1,4,3584]{2,1,0:T(4,128)S(1)} %dynamic-slice_bitcast_fusion), channel_id=2, replica_groups=mesh['section'=4,'tensor'=8] {'section'}, dimensions={0}, use_global_device_ids=true | all-gather | bytes 286720 | tf_op jit(solution)/shard_map/all_gather | solution.py:28
  94.4 1.5 %multiply_reduce_fusion = (f32[]{:T(128)}, f32[3584]{0:T(1024)}, f32[4,3584]{1,0:T(4,128)S(1)}) fusion(bf16[4,3584]{1,0:T(4,128)(2,1)S(1)} %copy-done.2, f32[4,3584]{1,0:T(4,128)S(1)} %reduce_sum.54, f32[3584]{0:T(1024)} %param.9), kind=kLoop, calls=%fused_computation.11 | loop fusion | flops 82431 | bytes 172036 | tf_op jit(solution)/shard_map/reduce_sum | solution.py:31
  95.9 0.0 copy-start.3
  95.9 9.5 %all-gather.3 = bf16[8,4,3584]{2,1,0:T(4,128)(2,1)} all-gather(bf16[1,4,3584]{2,1,0:T(4,128)(2,1)S(1)} %convert_bitcast_fusion), channel_id=1, replica_groups=mesh['section'=4,'tensor'=8] {'tensor'}, dimensions={0}, use_global_device_ids=true | all-gather | bytes 258048 | tf_op jit(solution)/shard_map/all_gather | solution.py:32
  105.5 1.0 reshape.27
  106.5 1.2 convolution_add_fusion.1
  107.6 0.0 copy-start.4
  107.6 1.8 %fusion = bf16[224,3584]{1,0:T(8,128)(2,1)} fusion(bf16[32,224]{1,0:T(8,128)(2,1)S(1)} %get-tuple-element.12, bf16[32,3584]{1,0:T(8,128)(2,1)S(1)} %reshape.27, bf16[224,3584]{1,0:T(8,128)(2,1)S(1)} %copy-done.1, f32[224]{0:T(256)S(1)} %add_sqrt_fusion, f32[224]{0:T(256)S(1)} %get-tuple-element.8), kind=kOutput, calls=%fused_computation.1 | convolution fusion | flops 55394304 | bytes 3456768 | tf_op jit(solution)/shard_map/dot_general | solution.py:35
  109.4 0.0 copy-done.3
  109.4 0.0 copy-done.4
  109.4 24.8 %all-reduce.1 = (f32[3584]{0:T(1024)}, f32[]{:T(128)}) all-reduce(f32[3584]{0:T(1024)S(1)} %copy-done.4, f32[]{:T(128)} %get-tuple-element.5), channel_id=1, replica_groups=mesh['section'=4,'tensor'=8] {'tensor'}, use_global_device_ids=true, to_apply=%region_5.0 | all-reduce | flops 3585 | bytes 28680 | tf_op jit(solution)/shard_map/psum | solution.py:31
  (3 shorter events, 0.1 us)
Async XLA Ops:
  7.2 15.0 %copy-start = (bf16[224,3584]{1,0:T(8,128)(2,1)S(1)}, bf16[224,3584]{1,0:T(8,128)(2,1)}, u32[]{:S(2)}) copy-start(bf16[224,3584]{1,0:T(8,128)(2,1)} %param.6) | copy-start | bytes 4816900
  7.2 2.0 %copy-start.2 = (bf16[4,3584]{1,0:T(4,128)(2,1)S(1)}, bf16[4,3584]{1,0:T(4,128)(2,1)}, u32[]{:S(2)}) copy-start(bf16[4,3584]{1,0:T(4,128)(2,1)} %param.5) | copy-start | bytes 86020
  7.2 15.0 %copy-start.5 = (f32[224]{0:T(256)S(1)}, f32[224]{0:T(256)}, u32[]{:S(2)}) copy-start(f32[224]{0:T(256)} %param.7) | copy-start | bytes 2692
  7.2 72.5 %all-reduce.4.cloned.1.call-start = ((), (), s32[]{:S(2)}) async-start(), calls=%async_computation | async-start | bytes 917504
  9.2 14.2 %copy-start.1 = (bf16[224,3584]{1,0:T(8,128)(2,1)S(1)}, bf16[224,3584]{1,0:T(8,128)(2,1)}, u32[]{:S(2)}) copy-start(bf16[224,3584]{1,0:T(8,128)(2,1)} %param.8) | copy-start | bytes 4816900
  23.4 41.1 %copy-start.6 = (u32[32]{0:T(128)S(1)}, u32[32]{0:T(128)}, u32[]{:S(2)}) copy-start(u32[32]{0:T(128)} %constant.13) | copy-start | bytes 388
  95.9 13.5 %copy-start.3 = (f32[4,3584]{1,0:T(4,128)}, f32[4,3584]{1,0:T(4,128)S(1)}, u32[]{:S(2)}) copy-start(f32[4,3584]{1,0:T(4,128)S(1)} %get-tuple-element.11) | copy-start | bytes 172036
  107.6 1.8 %copy-start.4 = (f32[3584]{0:T(1024)S(1)}, f32[3584]{0:T(1024)}, u32[]{:S(2)}) copy-start(f32[3584]{0:T(1024)} %get-tuple-element.6) | copy-start | bytes 43012
Sparse Core Ops, SparseCore 0:
  24.7 54.9 all-reduce.3
